TPU v7x, 32 devices: a whole 2x2x4 slice. The times are simulated.
32 devices in a mesh: expert: 16 (over z, y, x), replica: 2 (over core).
Axes of the slice: x: 2, y: 2, z: 4, core: 2. Of those that a mesh axis runs over, the one named last changes fastest.
Arguments:
- tokens: bfloat16 [1024, 7168], P('expert', 'replica'), may hold values from -6 to 6
- routes: int32 [1024, 8], P('expert'), may hold values from 0 to 15, all different within a row; in each aligned block of 64 rows (0 to 63, 64 to 127, ...) at most 64 rows name the same one
- route_scores: float32 [1024, 8], P('expert'), may hold values from 0.05 to 1
- placement: int32 [16], replicated, may hold values from 0 to 15, each once
- w_in: bfloat16 [16, 7168, 2, 1024], P('expert', 'replica'), may hold values from -0.0625 to 0.0625
- w_out: bfloat16 [16, 1024, 7168], P('expert', None, 'replica'), may hold values from -0.1875 to 0.1875
Outputs:
- mixed: bfloat16 [1024, 7168], P('expert', 'replica')
Inputs may be any that keep to these rules, and one draw needn't show every extreme that they name: `routes`: each row names 8 different logical experts. Among the 64 rows of each aligned block (the tokens of one index of the expert axis) no expert is named by more than 64 rows, a bound that some block reaches. `placement`: A permutation of the physical slots.
All inputs are finite; a program needn't handle non-finite values.
Results may differ from a plain program's by a relative error of at most 0.0057.
Values may be sent and summed in bfloat16 or wider, within the bound.
A program may use at most 128 MiB of HBM per device.

v0:
```python
import jax
import jax.numpy as jnp
from jax import lax
from jax.sharding import PartitionSpec as P


def packed(tokens, routes, route_scores, placement, w_in, w_out):
    tok_rows, feature_cols = tokens.shape
    route_count = routes.shape[1]
    experts = placement.shape[0]
    hidden_units = w_in.shape[3]
    capacity = min(tok_rows, max(2, 2 * tok_rows * route_count // experts))
    slot_total = experts * capacity
    expert_ids = jnp.arange(experts, dtype=jnp.int32)
    route_table = routes[:, :, None] == expert_ids
    physical = jnp.sum(jnp.where(route_table, placement, 0), axis=-1)
    flat_slots = physical.reshape(-1)
    onehot = (flat_slots[:, None] == expert_ids).astype(jnp.int32)
    earlier = jnp.sum((jnp.cumsum(onehot, axis=0) - onehot) * onehot, axis=1)
    position = (flat_slots * capacity + earlier).reshape(tok_rows, route_count)
    slot_index = jnp.arange(slot_total, dtype=jnp.int32)
    placing = jnp.any(position[None, :, :] == slot_index[:, None, None], axis=-1).astype(
        jnp.bfloat16
    )
    outgoing = jnp.dot(placing, tokens, preferred_element_type=jnp.float32).astype(jnp.bfloat16)
    incoming = lax.all_to_all(outgoing, "expert", split_axis=0, concat_axis=0, tiled=True)
    weights_in = w_in[0].reshape(feature_cols, 2 * hidden_units)
    weights_out = w_out[0]
    partial_value = jnp.dot(incoming, weights_in, preferred_element_type=jnp.float32)
    partial_value = partial_value.reshape(slot_total, 2, hidden_units)
    shares = lax.psum_scatter(partial_value, "replica", scatter_dimension=2, tiled=True)
    active = (jax.nn.silu(shares[:, 0]) * shares[:, 1]).astype(jnp.bfloat16)
    result = jnp.dot(
        lax.all_gather(active, "replica", axis=1, tiled=True),
        weights_out,
        preferred_element_type=jnp.float32,
    )
    expert_out = result.astype(jnp.bfloat16)
    returned = lax.all_to_all(expert_out, "expert", split_axis=0, concat_axis=0, tiled=True)
    route_weight = 2.5 * route_scores / jnp.sum(route_scores, axis=1, keepdims=True)
    picked = returned[position.reshape(-1)].reshape(tok_rows, route_count, feature_cols)
    mixed = jnp.sum(picked.astype(jnp.float32) * route_weight[:, :, None], axis=1)
    return mixed.astype(jnp.bfloat16)


def expert_weights(routes, route_scores, placement):
    experts = placement.shape[0]
    expert_ids = jnp.arange(experts, dtype=jnp.int32)
    physical = jnp.sum(jnp.where(routes[:, :, None] == expert_ids, placement, 0), axis=-1)
    route_weight = 2.5 * route_scores / jnp.sum(route_scores, axis=1, keepdims=True)
    return jnp.sum(
        jnp.where(physical[:, :, None] == expert_ids, route_weight[:, :, None], 0.0), axis=1
    )


def dense(tokens, routes, route_scores, placement, w_in, w_out):
    feature_cols = tokens.shape[1]
    hidden_units = w_in.shape[3]
    table = expert_weights(routes, route_scores, placement)
    mine = lax.all_to_all(table, "expert", split_axis=1, concat_axis=0, tiled=True)
    incoming = lax.all_gather(tokens, "expert", axis=0, tiled=True)
    rows = incoming.shape[0]
    weights_in = w_in[0].reshape(feature_cols, 2 * hidden_units)
    partial_value = jnp.dot(incoming, weights_in, preferred_element_type=jnp.float32)
    partial_value = partial_value.reshape(rows, 2, hidden_units)
    shares = lax.psum_scatter(partial_value, "replica", scatter_dimension=2, tiled=True)
    active = (jax.nn.silu(shares[:, 0]) * shares[:, 1]).astype(jnp.bfloat16)
    result = jnp.dot(
        lax.all_gather(active, "replica", axis=1, tiled=True),
        w_out[0],
        preferred_element_type=jnp.float32,
    )
    weighted = (result.astype(jnp.bfloat16).astype(jnp.float32) * mine).astype(jnp.bfloat16)
    return lax.psum_scatter(weighted, "expert", scatter_dimension=0, tiled=True)


def on_device(tokens, routes, route_scores, placement, w_in, w_out):
    tok_rows = tokens.shape[0]
    if 2 * tok_rows * routes.shape[1] // placement.shape[0] >= tok_rows:
        return dense(tokens, routes, route_scores, placement, w_in, w_out)
    return packed(tokens, routes, route_scores, placement, w_in, w_out)


def solution(mesh):
    in_specs = (
        P("expert", "replica"),
        P("expert", None),
        P("expert", None),
        P(),
        P("expert", "replica", None, None),
        P("expert", None, "replica"),
    )
    out_specs = P("expert", "replica")
    return jax.shard_map(
        on_device, mesh=mesh, in_specs=in_specs, out_specs=out_specs, check_vma=False
    )
```

profile of v0, /device:TPU:10, one launch (start us, length us, event | category | flops | bytes accessed | tf_op | source)
XLA Modules:
  0.0 345.8 jit_solution(17655661760736529164)
XLA Ops:
  6.5 0.0 all-gather.3.cloned.1.call-start
  6.5 0.7 all-gather.3.cloned.1.call-update
  7.3 0.0 reduce-scatter.3.cloned.1.call-start
  7.3 16.1 %copy.18 = bf16[448,8,2,1024]{3,1,2,0:T(8,128)(2,1)} copy(bf16[448,8,2,1024]{3,2,1,0:T(2,128)(2,1)} %bitcast.32) | data formatting | bytes 29360128
  23.4 18.9 %copy.16 = bf16[2048,3584]{1,0:T(8,128)(2,1)} copy(bf16[2048,3584]{0,1:T(8,128)(2,1)} %bitcast.31) | data formatting | bytes 29360128 | tf_op jit(solution)/shard_map/dot_general | solution.py:64
  42.3 71.1 %all-gather.3.cloned.1.call-done = bf16[1024,3584]{1,0:T(8,128)(2,1)} async-done(((bf16[64,3584]{1,0:T(8,128)(2,1)}), bf16[1024,3584]{1,0:T(8,128)(2,1)}) %all-gather.3.cloned.1.call-update) | async-done | bytes 7340048 | tf_op jit(solution)/shard_map/all_gather | solution.py:61
  113.4 21.6 %fusion.3 = f32[1024,2,1024]{2,0,1:T(8,128)} fusion(bf16[2,1024,3584]{2,1,0:T(8,128)(2,1)} %bitcast.33, bf16[1024,3584]{1,0:T(8,128)(2,1)} %all-gather.3.cloned.1.call-done), kind=kOutput, calls=%fused_computation.3 | convolution fusion | flops 15032385536 | bytes 30408704 | tf_op jit(solution)/shard_map/dot_general | solution.py:64
  135.0 0.0 copy-start
  135.0 0.0 copy-start.1
  135.0 0.0 copy-start.2
  135.0 0.0 reduce-scatter.3.cloned.1.call-update
  135.0 0.0 all-gather.5.cloned.1.call-start
  135.0 15.7 %reduce-scatter.3.cloned.1.call-done = f32[1024,2,512]{2,0,1:T(8,128)} async-done(((f32[1024,2,1024]{2,0,1:T(8,128)}), f32[1024,2,512]{2,0,1:T(8,128)}) %reduce-scatter.3.cloned.1.call-update) | async-done | bytes 4194320 | tf_op jit(solution)/shard_map/reduce_scatter | solution.py:66
  150.7 3.8 %fusion.6 = bf16[1024,512]{1,0:T(8,128)(2,1)} fusion(f32[1024,2,512]{2,0,1:T(8,128)} %reduce-scatter.3.cloned.1.call-done), kind=kLoop, calls=%fused_computation.7 | loop fusion | flops 3145728 | bytes 5242880 | tf_op jit(solution)/shard_map/convert_element_type | solution.py:67
  154.5 0.0 all-gather.5.cloned.1.call-update
  154.6 0.0 reduce-scatter.5.cloned.1.call-start
  154.6 0.0 copy-done
  154.7 0.0 copy-done.1
  154.7 0.0 copy-done.2
  154.7 0.1 select_reduce_fusion.1
  154.8 11.8 %all_to_all.16 = f32[64,16,1]{0,2,1:T(1,128)S(1)} all-to-all(f32[64,16,1]{0,2,1:T(1,128)S(1)} %bitcast.34), channel_id=1, replica_groups=mesh['expert'=16,'replica'=2] {'expert'}, dimensions={1} | all-to-all | bytes 8192 | tf_op jit(solution)/shard_map/all_to_all | solution.py:60
  166.7 0.1 mul.27
  166.7 0.0 all-gather.5.cloned.1.call-done
  166.7 12.5 %multiply_convert_fusion = bf16[1024,3584]{1,0:T(8,128)(2,1)} fusion(bf16[1024,1024]{1,0:T(8,128)(2,1)} %all-gather.5.cloned.1.call-done, bf16[1,1024,3584]{2,1,0:T(8,128)(2,1)} %param.11, f32[1024]{0:T(1024)S(1)} %mul.27), kind=kOutput, calls=%fused_computation | convolution fusion | flops 7530872832 | bytes 16781312 | tf_op jit(solution)/shard_map/dot_general | solution.py:68
  179.2 0.0 reduce-scatter.5.cloned.1.call-update
  179.3 160.0 %reduce-scatter.5.cloned.1.call-done = bf16[64,3584]{1,0:T(8,128)(2,1)} async-done(((bf16[1024,3584]{1,0:T(8,128)(2,1)}), bf16[64,3584]{1,0:T(8,128)(2,1)}) %reduce-scatter.5.cloned.1.call-update) | async-done | bytes 458768 | tf_op jit(solution)/shard_map/reduce_scatter | solution.py:74
  (4 shorter events, 0.1 us)
Async XLA Ops:
  6.5 106.8 %all-gather.3.cloned.1.call-start = ((), (), s32[]{:S(2)}) async-start(), calls=%async_computation.3 | async-start | bytes 7798784 | tf_op jit(solution)/shard_map/all_gather | solution.py:61
  7.3 143.4 %reduce-scatter.3.cloned.1.call-start = ((), (), s32[]{:S(2)}) async-start(), calls=%async_computation.4 | async-start | bytes 12582912 | tf_op jit(solution)/shard_map/reduce_scatter | solution.py:66
  135.0 19.7 %copy-start = (f32[64,8]{0,1:T(8,128)S(1)}, f32[64,8]{0,1:T(8,128)}, u32[]{:S(2)}) copy-start(f32[64,8]{0,1:T(8,128)} %param.8) | copy-start | bytes 6148
  135.0 19.7 %copy-start.1 = (s32[64,8]{0,1:T(8,128)S(1)}, s32[64,8]{0,1:T(8,128)}, u32[]{:S(2)}) copy-start(s32[64,8]{0,1:T(8,128)} %param.7) | copy-start | bytes 6148
  135.0 19.7 %copy-start.2 = (s32[16]{0:T(128)S(1)}, s32[16]{0:T(128)}, u32[]{:S(2)}) copy-start(s32[16]{0:T(128)} %param.9) | copy-start | bytes 196
  135.0 31.7 %all-gather.5.cloned.1.call-start = ((), (), s32[]{:S(2)}) async-start(), calls=%async_computation.5 | async-start | bytes 3145728 | tf_op jit(solution)/shard_map/all_gather | solution.py:69
  154.6 184.7 %reduce-scatter.5.cloned.1.call-start = ((), (), s32[]{:S(2)}) async-start(), calls=%async_computation.6 | async-start | bytes 7798784 | tf_op jit(solution)/shard_map/reduce_scatter | solution.py:74
Sparse Core Ops, SparseCore 0:
  10.0 103.2 all-gather.2
  135.1 15.5 reduce-scatter.2
  154.7 11.7 all-gather.4
  179.4 159.8 reduce-scatter.4
where the time goes:
time: 347 us; the launch traced here: 346 us
  waiting for transfers between devices  248 us (71%)
  local copies, waits for them, and re-layouts  35.1 us (10%)
  matrix products  34.1 us (10%)
  between operations  13.2 us (4%)
  blocking collectives  11.8 us (3%)
  other arithmetic  3.98 us (1%)
    reduce_scatter x1, waiting for transfers between devices, dense(): return lax.psum_scatter(weighted, 'expert', scatter_dimension=0, tiled=True)  160 us
    all_gather x1, waiting for transfers between devices, dense(): incoming = lax.all_gather(tokens, 'expert', axis=0, tiled=True)  71.1 us
    dot_general x1, matrix products, dense(): jnp.dot(incoming, weights_in, preferred_element_type=jnp.float32)  21.6 us
    dot_general x1, local copies, waits for them, and re-layouts, dense(): jnp.dot(incoming, weights_in, preferred_element_type=jnp.float32)  18.9 us
    unnamed x7, local copies, waits for them, and re-layouts  16.1 us
    reduce_scatter x1, waiting for transfers between devices, dense(): lax.psum_scatter(partial_value, 'replica', scatter_dimension=2, tiled=True)  15.7 us
    dot_general x1, matrix products, dense(): jnp.dot(lax.all_gather(active, 'replica', axis=1, tiled=True), w_out[0],...  12.5 us
    all_to_all x1, blocking collectives, dense(): lax.all_to_all(table, 'expert', split_axis=1, concat_axis=0, tiled=True)  11.8 us
  transfers between devices with their start and end apart: 4, of which 3 were waited for; matrix products, arithmetic and copies ran while one was open for 10% of the time, Pallas kernels for 0%

commit v1 on v0

--- a/solution.py
+++ b/solution.py
@@ -58,7 +58,14 @@
     hidden_units = w_in.shape[3]
     table = expert_weights(routes, route_scores, placement)
     mine = lax.all_to_all(table, "expert", split_axis=1, concat_axis=0, tiled=True)
-    incoming = lax.all_gather(tokens, "expert", axis=0, tiled=True)
+    size = lax.axis_size("expert")
+    forward = [(i, (i + 1) % size) for i in range(size)]
+    blocks = [tokens]
+    for stride in range(1, size):
+        blocks = [lax.ppermute(blocks[0], "expert", forward), *blocks]
+    result_2 = jnp.concatenate(blocks, axis=0)
+    shift = (lax.axis_index("expert") + 1) * blocks[-1].shape[0]
+    incoming = jnp.roll(result_2, shift, axis=0)
     rows = incoming.shape[0]
     weights_in = w_in[0].reshape(feature_cols, 2 * hidden_units)
     partial_value = jnp.dot(incoming, weights_in, preferred_element_type=jnp.float32)

time: 347 us -> 503 us (1.45)
  waiting for transfers between devices: 248 us -> 369 us
  local copies, waits for them, and re-layouts: 35.1 us -> 61.4 us
  starting transfers between devices: 0.12 us -> 10.5 us
    ppermute x0 -> x15, waiting for transfers between devices: none -> 168 us  [dense(): blocks = [lax.ppermute(blocks[0], 'expert', forward), *blocks]]
    all_gather x1 -> x0, waiting for transfers between devices: 71.1 us -> none  [dense(): incoming = lax.all_gather(tokens, 'expert', axis=0, tiled=True)]
    unnamed x7 -> x68, local copies, waits for them, and re-layouts: 16.1 us -> 42.5 us
    reduce_scatter x1, waiting for transfers between devices: 15.7 us -> 41.1 us  [dense(): lax.psum_scatter(partial_value, 'replica', scatter_dimension=2, tiled=True)]
    ppermute x0 -> x15, starting transfers between devices: none -> 10.4 us  [dense(): blocks = [lax.ppermute(blocks[0], 'expert', forward), *blocks]]
  transfers between devices with their start and end apart: 4 -> 18, of which waited for: 3 -> 16; matrix products, arithmetic and copies ran while one was open for 10% -> 7% of each run, Pallas kernels for 0% -> 0%
where the time goes in v1:
time: 503 us; the launch traced here: 502 us
  waiting for transfers between devices  369 us (73%)
  local copies, waits for them, and re-layouts  61.4 us (12%)
  matrix products  31.8 us (6%)
  between operations  13.5 us (3%)
  blocking collectives  11.8 us (2%)
  starting transfers between devices  10.5 us (2%)
    ppermute x15, waiting for transfers between devices, dense(): blocks = [lax.ppermute(blocks[0], 'expert', forward), *blocks]  168 us
    reduce_scatter x1, waiting for transfers between devices, dense(): return lax.psum_scatter(weighted, 'expert', scatter_dimension=0, tiled=True)  160 us
    unnamed x68, local copies, waits for them, and re-layouts  42.5 us
    reduce_scatter x1, waiting for transfers between devices, dense(): lax.psum_scatter(partial_value, 'replica', scatter_dimension=2, tiled=True)  41.1 us
    dot_general x1, matrix products, dense(): jnp.dot(incoming, weights_in, preferred_element_type=jnp.float32)  19.3 us
    dot_general x1, local copies, waits for them, and re-layouts, dense(): jnp.dot(incoming, weights_in, preferred_element_type=jnp.float32)  18.8 us
    dot_general x1, matrix products, dense(): jnp.dot(lax.all_gather(active, 'replica', axis=1, tiled=True), w_out[0],...  12.5 us
    all_to_all x1, blocking collectives, dense(): lax.all_to_all(table, 'expert', split_axis=1, concat_axis=0, tiled=True)  11.8 us
  transfers between devices with their start and end apart: 18, of which 16 were waited for; matrix products, arithmetic and copies ran while one was open for 7% of the time, Pallas kernels for 0%

profile of v1, /device:TPU:10, one launch (start us, length us, event | category | flops | bytes accessed | tf_op | source)
XLA Modules:
  0.0 501.8 jit_solution(6012919315221202801)
XLA Ops:
  6.5 1.5 collective-permute-start
  8.0 11.0 %collective-permute-done = bf16[64,3584]{1,0:T(8,128)(2,1)S(1)} collective-permute-done((bf16[64,3584]{1,0:T(8,128)(2,1)}, bf16[64,3584]{1,0:T(8,128)(2,1)S(1)}, u32[]{:S(2)}, u32[]{:S(2)}) %collective-permute-start) | collective-permute-done | bytes 458784 | tf_op jit(solution)/shard_map/ppermute | solution.py:65
  19.0 2.4 collective-permute-start.1
  21.4 9.6 %collective-permute-done.1 = bf16[64,3584]{1,0:T(8,128)(2,1)S(1)} collective-permute-done((bf16[64,3584]{1,0:T(8,128)(2,1)S(1)}, bf16[64,3584]{1,0:T(8,128)(2,1)S(1)}, u32[]{:S(2)}, u32[]{:S(2)}) %collective-permute-start.1) | collective-permute-done | bytes 458784 | tf_op jit(solution)/shard_map/ppermute | solution.py:65
  31.0 2.7 collective-permute-start.2
  33.7 9.6 %collective-permute-done.2 = bf16[64,3584]{1,0:T(8,128)(2,1)S(1)} collective-permute-done((bf16[64,3584]{1,0:T(8,128)(2,1)S(1)}, bf16[64,3584]{1,0:T(8,128)(2,1)S(1)}, u32[]{:S(2)}, u32[]{:S(2)}) %collective-permute-start.2) | collective-permute-done | bytes 458784 | tf_op jit(solution)/shard_map/ppermute | solution.py:65
  43.3 1.8 collective-permute-start.3
  45.1 9.7 %collective-permute-done.3 = bf16[64,3584]{1,0:T(8,128)(2,1)S(1)} collective-permute-done((bf16[64,3584]{1,0:T(8,128)(2,1)S(1)}, bf16[64,3584]{1,0:T(8,128)(2,1)S(1)}, u32[]{:S(2)}, u32[]{:S(2)}) %collective-permute-start.3) | collective-permute-done | bytes 458784 | tf_op jit(solution)/shard_map/ppermute | solution.py:65
  54.8 1.0 collective-permute-start.4
  55.8 9.7 %collective-permute-done.4 = bf16[64,3584]{1,0:T(8,128)(2,1)S(1)} collective-permute-done((bf16[64,3584]{1,0:T(8,128)(2,1)S(1)}, bf16[64,3584]{1,0:T(8,128)(2,1)S(1)}, u32[]{:S(2)}, u32[]{:S(2)}) %collective-permute-start.4) | collective-permute-done | bytes 458784 | tf_op jit(solution)/shard_map/ppermute | solution.py:65
  66.1 10.4 %collective-permute-done.5 = bf16[64,3584]{1,0:T(8,128)(2,1)S(1)} collective-permute-done((bf16[64,3584]{1,0:T(8,128)(2,1)S(1)}, bf16[64,3584]{1,0:T(8,128)(2,1)S(1)}, u32[]{:S(2)}, u32[]{:S(2)}) %collective-permute-start.5) | collective-permute-done | bytes 458784 | tf_op jit(solution)/shard_map/ppermute | solution.py:65
  76.9 11.4 %collective-permute-done.6 = bf16[64,3584]{1,0:T(8,128)(2,1)S(1)} collective-permute-done((bf16[64,3584]{1,0:T(8,128)(2,1)S(1)}, bf16[64,3584]{1,0:T(8,128)(2,1)S(1)}, u32[]{:S(2)}, u32[]{:S(2)}) %collective-permute-start.6) | collective-permute-done | bytes 458784 | tf_op jit(solution)/shard_map/ppermute | solution.py:65
  88.2 0.8 copy-done.2
  89.1 13.0 %collective-permute-done.7 = bf16[64,3584]{1,0:T(8,128)(2,1)S(1)} collective-permute-done((bf16[64,3584]{1,0:T(8,128)(2,1)S(1)}, bf16[64,3584]{1,0:T(8,128)(2,1)S(1)}, u32[]{:S(2)}, u32[]{:S(2)}) %collective-permute-start.7) | collective-permute-done | bytes 458784 | tf_op jit(solution)/shard_map/ppermute | solution.py:65
  102.0 0.8 copy-done.4
  102.8 14.1 %collective-permute-done.8 = bf16[64,3584]{1,0:T(8,128)(2,1)S(1)} collective-permute-done((bf16[64,3584]{1,0:T(8,128)(2,1)S(1)}, bf16[64,3584]{1,0:T(8,128)(2,1)S(1)}, u32[]{:S(2)}, u32[]{:S(2)}) %collective-permute-start.8) | collective-permute-done | bytes 458784 | tf_op jit(solution)/shard_map/ppermute | solution.py:65
  117.0 0.8 copy-done.6
  117.7 15.3 %collective-permute-done.9 = bf16[64,3584]{1,0:T(8,128)(2,1)S(1)} collective-permute-done((bf16[64,3584]{1,0:T(8,128)(2,1)S(1)}, bf16[64,3584]{1,0:T(8,128)(2,1)S(1)}, u32[]{:S(2)}, u32[]{:S(2)}) %collective-permute-start.9) | collective-permute-done | bytes 458784 | tf_op jit(solution)/shard_map/ppermute | solution.py:65
  133.1 0.8 copy-done.8
  133.8 14.6 %collective-permute-done.10 = bf16[64,3584]{1,0:T(8,128)(2,1)S(1)} collective-permute-done((bf16[64,3584]{1,0:T(8,128)(2,1)S(1)}, bf16[64,3584]{1,0:T(8,128)(2,1)S(1)}, u32[]{:S(2)}, u32[]{:S(2)}) %collective-permute-start.10) | collective-permute-done | bytes 458784 | tf_op jit(solution)/shard_map/ppermute | solution.py:65
  148.4 0.8 copy-done.10
  149.2 13.4 %collective-permute-done.11 = bf16[64,3584]{1,0:T(8,128)(2,1)S(1)} collective-permute-done((bf16[64,3584]{1,0:T(8,128)(2,1)S(1)}, bf16[64,3584]{1,0:T(8,128)(2,1)S(1)}, u32[]{:S(2)}, u32[]{:S(2)}) %collective-permute-start.11) | collective-permute-done | bytes 458784 | tf_op jit(solution)/shard_map/ppermute | solution.py:65
  162.6 0.8 copy-done.12
  163.4 12.5 %collective-permute-done.12 = bf16[64,3584]{1,0:T(8,128)(2,1)S(1)} collective-permute-done((bf16[64,3584]{1,0:T(8,128)(2,1)S(1)}, bf16[64,3584]{1,0:T(8,128)(2,1)S(1)}, u32[]{:S(2)}, u32[]{:S(2)}) %collective-permute-start.12) | collective-permute-done | bytes 458784 | tf_op jit(solution)/shard_map/ppermute | solution.py:65
  175.9 0.8 copy-done.13
  176.7 13.4 %collective-permute-done.13 = bf16[64,3584]{1,0:T(8,128)(2,1)} collective-permute-done((bf16[64,3584]{1,0:T(8,128)(2,1)S(1)}, bf16[64,3584]{1,0:T(8,128)(2,1)}, u32[]{:S(2)}, u32[]{:S(2)}) %collective-permute-start.13) | collective-permute-done | bytes 458784 | tf_op jit(solution)/shard_map/ppermute | solution.py:65
  190.0 16.1 %copy.18 = bf16[448,8,2,1024]{3,1,2,0:T(8,128)(2,1)} copy(bf16[448,8,2,1024]{3,2,1,0:T(2,128)(2,1)} %bitcast.32) | data formatting | bytes 29360128
  206.1 18.8 %copy.16 = bf16[2048,3584]{1,0:T(8,128)(2,1)} copy(bf16[2048,3584]{0,1:T(8,128)(2,1)} %bitcast.31) | data formatting | bytes 29360128 | tf_op jit(solution)/shard_map/dot_general | solution.py:71
  224.9 1.2 constant_dynamic-update-slice_fusion.31
  226.1 1.7 constant_dynamic-update-slice_fusion.30
  227.9 1.4 constant_dynamic-update-slice_fusion.29
  229.3 1.4 constant_dynamic-update-slice_fusion.28
  230.7 1.1 constant_dynamic-update-slice_fusion.27
  231.8 1.1 constant_dynamic-update-slice_fusion.26
  232.8 1.1 constant_dynamic-update-slice_fusion.25
  233.9 1.1 constant_dynamic-update-slice_fusion.24
  234.9 1.1 constant_dynamic-update-slice_fusion.23
  236.3 1.1 constant_dynamic-update-slice_fusion.15
  237.3 1.1 constant_dynamic-update-slice_fusion.14
  238.4 1.1 constant_dynamic-update-slice_fusion.13
  239.4 1.1 constant_dynamic-update-slice_fusion.12
  241.0 5.1 %copy-done.15 = bf16[2048,3584]{1,0:T(8,128)(2,1)} copy-done((bf16[2048,3584]{1,0:T(8,128)(2,1)}, bf16[2048,3584]{1,0:T(8,128)(2,1)S(1)}, u32[]{:S(2)}) %copy-start.15) | copy-done | bytes 14680088
  246.2 19.3 %fusion.3 = f32[1024,2,1024]{2,0,1:T(8,128)} fusion(bf16[2,1024,3584]{2,1,0:T(8,128)(2,1)S(1)} %bitcast.33, bf16[2048,3584]{1,0:T(8,128)(2,1)} %copy-done.15, s32[]{:T(128)S(6)} %select_n.22), kind=kOutput, calls=%fused_computation.3 | convolution fusion | flops 15032385536 | bytes 30408708 | tf_op jit(solution)/shard_map/dot_general | solution.py:71
  265.5 41.1 %reduce-scatter.3.cloned.1.call-done = f32[1024,2,512]{2,0,1:T(8,128)} async-done(((f32[1024,2,1024]{2,0,1:T(8,128)}), f32[1024,2,512]{2,0,1:T(8,128)}) %reduce-scatter.3.cloned.1.call-update) | async-done | bytes 4194320 | tf_op jit(solution)/shard_map/reduce_scatter | solution.py:73
  306.6 3.9 fusion.7
  310.7 11.8 %all_to_all.16 = f32[64,16,1]{0,2,1:T(1,128)S(1)} all-to-all(f32[64,16,1]{0,2,1:T(1,128)S(1)} %bitcast.34), channel_id=1, replica_groups=mesh['expert'=16,'replica'=2] {'expert'}, dimensions={1} | all-to-all | bytes 8192 | tf_op jit(solution)/shard_map/all_to_all | solution.py:60
  322.7 12.5 %multiply_convert_fusion = bf16[1024,3584]{1,0:T(8,128)(2,1)} fusion(bf16[1024,1024]{1,0:T(8,128)(2,1)} %all-gather.2.cloned.1.call-done, bf16[1,1024,3584]{2,1,0:T(8,128)(2,1)} %param.11, f32[1024]{0:T(1024)S(1)} %mul.31), kind=kOutput, calls=%fused_computation | convolution fusion | flops 7530872832 | bytes 16781312 | tf_op jit(solution)/shard_map/dot_general | solution.py:75
  335.2 160.0 %reduce-scatter.5.cloned.1.call-done = bf16[64,3584]{1,0:T(8,128)(2,1)} async-done(((bf16[1024,3584]{1,0:T(8,128)(2,1)}), bf16[64,3584]{1,0:T(8,128)(2,1)}) %reduce-scatter.5.cloned.1.call-update) | async-done | bytes 458768 | tf_op jit(solution)/shard_map/reduce_scatter | solution.py:81
  (71 shorter events, 2.0 us)
Async XLA Ops:
  6.5 300.1 %reduce-scatter.3.cloned.1.call-start = ((), (), s32[]{:S(2)}) async-start(), calls=%async_computation.3 | async-start | bytes 12582912 | tf_op jit(solution)/shard_map/reduce_scatter | solution.py:73
  6.5 12.5 %collective-permute-start = (bf16[64,3584]{1,0:T(8,128)(2,1)}, bf16[64,3584]{1,0:T(8,128)(2,1)S(1)}, u32[]{:S(2)}, u32[]{:S(2)}) collective-permute-start(bf16[64,3584]{1,0:T(8,128)(2,1)} %param.6), channel_id=1, source_target_pairs={{0,2},{2,4},{4,6},{6,8},{8,10},{10,12},{12,14},{14,16},{16,18},{18... | collective-permute-start | bytes 1376264 | tf_op jit(solution)/shard_map/ppermute | solution.py:65
  19.0 12.0 %collective-permute-start.1 = (bf16[64,3584]{1,0:T(8,128)(2,1)S(1)}, bf16[64,3584]{1,0:T(8,128)(2,1)S(1)}, u32[]{:S(2)}, u32[]{:S(2)}) collective-permute-start(bf16[64,3584]{1,0:T(8,128)(2,1)S(1)} %collective-permute-done), channel_id=1, source_target_pairs={{0,2},{2,4},{4,6},{6,8},{8,10},{10,12},{12,14},{14,16},{16,18},{18... | collective-permute-start | bytes 1376264 | tf_op jit(solution)/shard_map/ppermute | solution.py:65
  31.0 12.3 %collective-permute-start.2 = (bf16[64,3584]{1,0:T(8,128)(2,1)S(1)}, bf16[64,3584]{1,0:T(8,128)(2,1)S(1)}, u32[]{:S(2)}, u32[]{:S(2)}) collective-permute-start(bf16[64,3584]{1,0:T(8,128)(2,1)S(1)} %collective-permute-done.1), channel_id=1, source_target_pairs={{0,2},{2,4},{4,6},{6,8},{8,10},{10,12},{12,14},{14,16},{16,18},{18... | collective-permute-start | bytes 1376264 | tf_op jit(solution)/shard_map/ppermute | solution.py:65
  43.3 11.5 %collective-permute-start.3 = (bf16[64,3584]{1,0:T(8,128)(2,1)S(1)}, bf16[64,3584]{1,0:T(8,128)(2,1)S(1)}, u32[]{:S(2)}, u32[]{:S(2)}) collective-permute-start(bf16[64,3584]{1,0:T(8,128)(2,1)S(1)} %collective-permute-done.2), channel_id=1, source_target_pairs={{0,2},{2,4},{4,6},{6,8},{8,10},{10,12},{12,14},{14,16},{16,18},{18... | collective-permute-start | bytes 1376264 | tf_op jit(solution)/shard_map/ppermute | solution.py:65
  54.8 10.7 %collective-permute-start.4 = (bf16[64,3584]{1,0:T(8,128)(2,1)S(1)}, bf16[64,3584]{1,0:T(8,128)(2,1)S(1)}, u32[]{:S(2)}, u32[]{:S(2)}) collective-permute-start(bf16[64,3584]{1,0:T(8,128)(2,1)S(1)} %collective-permute-done.3), channel_id=1, source_target_pairs={{0,2},{2,4},{4,6},{6,8},{8,10},{10,12},{12,14},{14,16},{16,18},{18... | collective-permute-start | bytes 1376264 | tf_op jit(solution)/shard_map/ppermute | solution.py:65
  65.5 10.9 %collective-permute-start.5 = (bf16[64,3584]{1,0:T(8,128)(2,1)S(1)}, bf16[64,3584]{1,0:T(8,128)(2,1)S(1)}, u32[]{:S(2)}, u32[]{:S(2)}) collective-permute-start(bf16[64,3584]{1,0:T(8,128)(2,1)S(1)} %collective-permute-done.4), channel_id=1, source_target_pairs={{0,2},{2,4},{4,6},{6,8},{8,10},{10,12},{12,14},{14,16},{16,18},{18... | collective-permute-start | bytes 1376264 | tf_op jit(solution)/shard_map/ppermute | solution.py:65
  76.4 11.8 %collective-permute-start.6 = (bf16[64,3584]{1,0:T(8,128)(2,1)S(1)}, bf16[64,3584]{1,0:T(8,128)(2,1)S(1)}, u32[]{:S(2)}, u32[]{:S(2)}) collective-permute-start(bf16[64,3584]{1,0:T(8,128)(2,1)S(1)} %collective-permute-done.5), channel_id=1, source_target_pairs={{0,2},{2,4},{4,6},{6,8},{8,10},{10,12},{12,14},{14,16},{16,18},{18... | collective-permute-start | bytes 1376264 | tf_op jit(solution)/shard_map/ppermute | solution.py:65
  88.2 0.8 copy-start.2
  89.1 13.0 %collective-permute-start.7 = (bf16[64,3584]{1,0:T(8,128)(2,1)S(1)}, bf16[64,3584]{1,0:T(8,128)(2,1)S(1)}, u32[]{:S(2)}, u32[]{:S(2)}) collective-permute-start(bf16[64,3584]{1,0:T(8,128)(2,1)S(1)} %collective-permute-done.6), channel_id=1, source_target_pairs={{0,2},{2,4},{4,6},{6,8},{8,10},{10,12},{12,14},{14,16},{16,18},{18... | collective-permute-start | bytes 1376264 | tf_op jit(solution)/shard_map/ppermute | solution.py:65
  102.0 0.8 copy-start.4
  102.8 14.1 %collective-permute-start.8 = (bf16[64,3584]{1,0:T(8,128)(2,1)S(1)}, bf16[64,3584]{1,0:T(8,128)(2,1)S(1)}, u32[]{:S(2)}, u32[]{:S(2)}) collective-permute-start(bf16[64,3584]{1,0:T(8,128)(2,1)S(1)} %collective-permute-done.7), channel_id=1, source_target_pairs={{0,2},{2,4},{4,6},{6,8},{8,10},{10,12},{12,14},{14,16},{16,18},{18... | collective-permute-start | bytes 1376264 | tf_op jit(solution)/shard_map/ppermute | solution.py:65
  117.0 0.8 copy-start.6
  117.7 15.3 %collective-permute-start.9 = (bf16[64,3584]{1,0:T(8,128)(2,1)S(1)}, bf16[64,3584]{1,0:T(8,128)(2,1)S(1)}, u32[]{:S(2)}, u32[]{:S(2)}) collective-permute-start(bf16[64,3584]{1,0:T(8,128)(2,1)S(1)} %collective-permute-done.8), channel_id=1, source_target_pairs={{0,2},{2,4},{4,6},{6,8},{8,10},{10,12},{12,14},{14,16},{16,18},{18... | collective-permute-start | bytes 1376264 | tf_op jit(solution)/shard_map/ppermute | solution.py:65
  133.1 0.8 copy-start.8
  133.8 14.6 %collective-permute-start.10 = (bf16[64,3584]{1,0:T(8,128)(2,1)S(1)}, bf16[64,3584]{1,0:T(8,128)(2,1)S(1)}, u32[]{:S(2)}, u32[]{:S(2)}) collective-permute-start(bf16[64,3584]{1,0:T(8,128)(2,1)S(1)} %collective-permute-done.9), channel_id=1, source_target_pairs={{0,2},{2,4},{4,6},{6,8},{8,10},{10,12},{12,14},{14,16},{16,18},{18... | collective-permute-start | bytes 1376264 | tf_op jit(solution)/shard_map/ppermute | solution.py:65
  148.4 0.8 copy-start.10
  149.2 13.4 %collective-permute-start.11 = (bf16[64,3584]{1,0:T(8,128)(2,1)S(1)}, bf16[64,3584]{1,0:T(8,128)(2,1)S(1)}, u32[]{:S(2)}, u32[]{:S(2)}) collective-permute-start(bf16[64,3584]{1,0:T(8,128)(2,1)S(1)} %collective-permute-done.10), channel_id=1, source_target_pairs={{0,2},{2,4},{4,6},{6,8},{8,10},{10,12},{12,14},{14,16},{16,18},{18... | collective-permute-start | bytes 1376264 | tf_op jit(solution)/shard_map/ppermute | solution.py:65
  162.6 0.8 copy-start.12
  163.4 12.5 %collective-permute-start.12 = (bf16[64,3584]{1,0:T(8,128)(2,1)S(1)}, bf16[64,3584]{1,0:T(8,128)(2,1)S(1)}, u32[]{:S(2)}, u32[]{:S(2)}) collective-permute-start(bf16[64,3584]{1,0:T(8,128)(2,1)S(1)} %collective-permute-done.11), channel_id=1, source_target_pairs={{0,2},{2,4},{4,6},{6,8},{8,10},{10,12},{12,14},{14,16},{16,18},{18... | collective-permute-start | bytes 1376264 | tf_op jit(solution)/shard_map/ppermute | solution.py:65
  175.9 0.8 copy-start.13
  176.7 13.4 %collective-permute-start.13 = (bf16[64,3584]{1,0:T(8,128)(2,1)S(1)}, bf16[64,3584]{1,0:T(8,128)(2,1)}, u32[]{:S(2)}, u32[]{:S(2)}) collective-permute-start(bf16[64,3584]{1,0:T(8,128)(2,1)S(1)} %collective-permute-done.12), channel_id=1, source_target_pairs={{0,2},{2,4},{4,6},{6,8},{8,10},{10,12},{12,14},{14,16},{16,18},{18... | collective-permute-start | bytes 1376264 | tf_op jit(solution)/shard_map/ppermute | solution.py:65
  190.0 34.9 %collective-permute-start.14 = (bf16[64,3584]{1,0:T(8,128)(2,1)}, bf16[64,3584]{1,0:T(8,128)(2,1)}, u32[]{:S(2)}, u32[]{:S(2)}) collective-permute-start(bf16[64,3584]{1,0:T(8,128)(2,1)} %collective-permute-done.13), channel_id=1, source_target_pairs={{0,2},{2,4},{4,6},{6,8},{8,10},{10,12},{12,14},{14,16},{16,18},{18... | collective-permute-start | bytes 1376264 | tf_op jit(solution)/shard_map/ppermute | solution.py:65
  206.1 30.1 %copy-start.1 = (bf16[64,3584]{1,0:T(8,128)(2,1)S(1)}, bf16[64,3584]{1,0:T(8,128)(2,1)}, u32[]{:S(2)}) copy-start(bf16[64,3584]{1,0:T(8,128)(2,1)} %param.6) | copy-start | bytes 1376260
  224.9 15.6 %copy-start.11 = (bf16[64,3584]{1,0:T(8,128)(2,1)S(1)}, bf16[64,3584]{1,0:T(8,128)(2,1)}, u32[]{:S(2)}) copy-start(bf16[64,3584]{1,0:T(8,128)(2,1)} %copy-done.10) | copy-start | bytes 1376260
  224.9 15.7 %copy-start.9 = (bf16[64,3584]{1,0:T(8,128)(2,1)S(1)}, bf16[64,3584]{1,0:T(8,128)(2,1)}, u32[]{:S(2)}) copy-start(bf16[64,3584]{1,0:T(8,128)(2,1)} %copy-done.8) | copy-start | bytes 1376260
  224.9 15.7 %copy-start.7 = (bf16[64,3584]{1,0:T(8,128)(2,1)S(1)}, bf16[64,3584]{1,0:T(8,128)(2,1)}, u32[]{:S(2)}) copy-start(bf16[64,3584]{1,0:T(8,128)(2,1)} %copy-done.6) | copy-start | bytes 1376260
  224.9 15.8 %copy-start.5 = (bf16[64,3584]{1,0:T(8,128)(2,1)S(1)}, bf16[64,3584]{1,0:T(8,128)(2,1)}, u32[]{:S(2)}) copy-start(bf16[64,3584]{1,0:T(8,128)(2,1)} %copy-done.4) | copy-start | bytes 1376260
  224.9 15.8 %copy-start.3 = (bf16[64,3584]{1,0:T(8,128)(2,1)S(1)}, bf16[64,3584]{1,0:T(8,128)(2,1)}, u32[]{:S(2)}) copy-start(bf16[64,3584]{1,0:T(8,128)(2,1)} %copy-done.2) | copy-start | bytes 1376260
  224.9 21.3 %copy-start = (bf16[2048,3584]{1,0:T(8,128)(2,1)S(1)}, bf16[2048,3584]{1,0:T(8,128)(2,1)}, u32[]{:S(2)}) copy-start(bf16[2048,3584]{1,0:T(8,128)(2,1)} %copy.16) | copy-start | bytes 44040196
  241.0 5.1 %copy-start.15 = (bf16[2048,3584]{1,0:T(8,128)(2,1)}, bf16[2048,3584]{1,0:T(8,128)(2,1)S(1)}, u32[]{:S(2)}) copy-start(bf16[2048,3584]{1,0:T(8,128)(2,1)S(1)} %constant_dynamic-update-slice_fusion) | copy-start | bytes 44040196
  265.5 45.1 %copy-start.14 = (f32[64,8]{0,1:T(8,128)S(1)}, f32[64,8]{0,1:T(8,128)}, u32[]{:S(2)}) copy-start(f32[64,8]{0,1:T(8,128)} %param.8) | copy-start | bytes 6148
  265.5 45.1 %copy-start.16 = (s32[64,8]{0,1:T(8,128)S(1)}, s32[64,8]{0,1:T(8,128)}, u32[]{:S(2)}) copy-start(s32[64,8]{0,1:T(8,128)} %param.7) | copy-start | bytes 6148
  265.5 45.1 %copy-start.17 = (s32[16]{0:T(128)S(1)}, s32[16]{0:T(128)}, u32[]{:S(2)}) copy-start(s32[16]{0:T(128)} %param.9) | copy-start | bytes 196
  265.5 57.2 %all-gather.2.cloned.1.call-start = ((), (), s32[]{:S(2)}) async-start(), calls=%async_computation.4 | async-start | bytes 3145728 | tf_op jit(solution)/shard_map/all_gather | solution.py:76
  310.5 184.7 %reduce-scatter.5.cloned.1.call-start = ((), (), s32[]{:S(2)}) async-start(), calls=%async_computation.5 | async-start | bytes 7798784 | tf_op jit(solution)/shard_map/reduce_scatter | solution.py:81
Sparse Core Ops, SparseCore 0:
  265.6 40.9 reduce-scatter.2
  310.6 11.7 all-gather.1
  335.3 159.8 reduce-scatter.4
